TPU v7x, 32 devices: a whole 2x2x4 slice. The times are simulated.
32 devices in a mesh: chan: 8 (over z, x), band: 4 (over y, core).
Axes of the slice: x: 2, y: 2, z: 4, core: 2. Of those that a mesh axis runs over, the one named last changes fastest.
Arguments:
- spectra: bfloat16 [8, 2, 4096, 512], P('band', None, 'chan'), may hold values from -64 to 64
- half_width: int32 [512], replicated, may hold values from 1 to 32, as said below
- panel_block: int32 [4], replicated, may hold values from 0 to 7
- panel_offset: int32 [4], replicated, may hold values from 0 to 256
Outputs:
- cross: bfloat16 [4, 8, 2, 4096, 256], P(None, 'band', None, 'chan')
Inputs may be any that keep to these rules, and one draw needn't show every extreme that they name: `half_width`: some window's half-width is exactly 32.
All inputs are finite; a program needn't handle non-finite values.
Results may differ from a plain program's by a relative error of at most 0.0056.
Values may be sent and summed in bfloat16 or wider, within the bound.
No kernel may reach another device: no remote copies, remote signals or barrier semaphores. Data moves between devices by JAX's collectives and lax.ppermute only.
A program may use at most 64 MiB of HBM per device.

v0:
```python
import jax
import jax.numpy as jnp
from jax import lax
from jax.sharding import PartitionSpec as P

PANEL = 256
NPANEL = 4
HALO = 32


def with_halo(block, sides, width):
    for axis, dim in sides:
        count = lax.axis_size(axis)
        forward = [(i, i + 1) for i in range(count - 1)]
        backward = [(target, source) for source, target in forward]
        low = lax.ppermute(
            lax.slice_in_dim(block, block.shape[dim] - width, None, axis=dim), axis, forward
        )
        high = lax.ppermute(lax.slice_in_dim(block, 0, width, axis=dim), axis, backward)
        block = jnp.concatenate([low, block, high], axis=dim)
    return block


def from_root(block, axis, holder):
    block = jnp.where(lax.axis_index(axis) == holder, block, jnp.zeros_like(block))
    return lax.psum(block, axis)


def norm_scale(power, widths, first_chan, channels, bins):
    rows = power.shape[0]
    padded = with_halo(power, (("chan", 0),), HALO)
    total = jnp.zeros_like(power)
    for offset in range(-HALO, HALO + 1):
        window = padded[HALO + offset : HALO + offset + rows]
        total = total + jnp.where(abs(offset) <= widths[None, :], window, jnp.float32(0.0))
    chan_index = jnp.arange(rows, dtype=jnp.int32)[:, None] + first_chan
    count = (
        jnp.minimum(chan_index + widths[None, :], channels - 1)
        - jnp.maximum(chan_index - widths[None, :], 0)
        + 1
    )
    return lax.rsqrt(total / (count.astype(jnp.float32) * bins) + 1e-06)


def local(spectra, half_width, panel_block, panel_offset):
    f_dev, parts, ch_dev, windows = spectra.shape
    bins = f_dev * lax.axis_size("band")
    channels = ch_dev * lax.axis_size("chan")
    block_here = lax.axis_index("chan")
    first_chan = block_here * ch_dev
    local_power = jnp.sum(jnp.square(spectra.astype(jnp.float32)), axis=(0, 1))
    share = lax.psum_scatter(local_power, "band", scatter_dimension=1, tiled=True)
    share_width = share.shape[1]
    widths = lax.dynamic_slice_in_dim(half_width, lax.axis_index("band") * share_width, share_width)
    scale_share = norm_scale(share, widths, first_chan, channels, bins)
    scale = lax.all_gather(scale_share, "band", axis=1, tiled=True)
    normed = (spectra.astype(jnp.float32) * scale[None, None]).astype(jnp.bfloat16)
    flat = normed.reshape(f_dev, 2 * ch_dev, windows)
    results = []
    for panel in range(NPANEL):
        source = from_root(
            lax.dynamic_slice_in_dim(normed, panel_offset[panel], PANEL, 2),
            "chan",
            panel_block[panel],
        )
        right = source.reshape(f_dev, 2 * PANEL, windows)
        grams = jnp.einsum("fxw,fyw->fxy", flat, right, preferred_element_type=jnp.float32)
        real_part = grams[:, :ch_dev, :PANEL] + grams[:, ch_dev:, PANEL:]
        imag_part = grams[:, ch_dev:, :PANEL] - grams[:, :ch_dev, PANEL:]
        results.append(
            (jnp.stack([real_part, imag_part], axis=1) * windows ** (-0.5)).astype(jnp.bfloat16)
        )
    return jnp.stack(results)


def solution(mesh):
    placed = (P("band", None, "chan", None), P(), P(), P())
    return jax.shard_map(
        local,
        mesh=mesh,
        in_specs=placed,
        out_specs=P(None, "band", None, "chan", None),
        check_vma=False,
    )
```

profile of v0, /device:TPU:0, one launch (start us, length us, event | category | flops | bytes accessed | tf_op | source)
XLA Modules:
  0.0 251.9 jit_solution(6635391899001738447)
XLA Ops:
  6.5 0.0 reduce-scatter.2.cloned.1.call-start
  6.5 3.1 %fusion = f32[512,512]{1,0:T(8,128)} fusion(bf16[2,2,512,512]{3,2,1,0:T(8,128)(2,1)} %param.4), kind=kLoop, calls=%fused_computation.2 | loop fusion | flops 2883584 | bytes 3145728 | tf_op jit(solution)/shard_map/reduce_sum | solution.py:51
  9.6 0.0 reduce-scatter.2.cloned.1.call-update
  9.7 0.0 all-gather.2.cloned.1.call-start
  9.7 0.8 broadcast_compare_fusion.32
  10.5 26.9 %reduce-scatter.2.cloned.1.call-done = f32[512,128]{1,0:T(8,128)} async-done(((f32[512,512]{1,0:T(8,128)}), f32[512,128]{1,0:T(8,128)}) %reduce-scatter.2.cloned.1.call-update) | async-done | bytes 262160 | tf_op jit(solution)/shard_map/reduce_scatter | solution.py:52
  37.4 0.7 fusion.81
  38.1 3.3 %collective-permute-start = (f32[32,128]{1,0:T(8,128)S(1)}, f32[32,128]{1,0:T(8,128)S(1)}, u32[]{:S(2)}, u32[]{:S(2)}) collective-permute-start(f32[32,128]{1,0:T(8,128)S(1)} %get-tuple-element.25), channel_id=1, source_target_pairs={{0,4},{4,8},{8,12},{12,16},{16,20},{20,24},{24,28},{1,5},{5,9},{9,... | collective-permute-start | bytes 49160 | tf_op jit(solution)/shard_map/ppermute | solution.py:16
  41.5 1.3 collective-permute-start.1
  42.8 0.1 collective-permute-done
  42.9 1.0 constant_dynamic-update-slice_fusion
  43.9 3.2 %collective-permute-done.1 = f32[32,128]{1,0:T(8,128)S(1)} collective-permute-done((f32[32,128]{1,0:T(8,128)S(1)}, f32[32,128]{1,0:T(8,128)S(1)}, u32[]{:S(2)}, u32[]{:S(2)}) %collective-permute-start.1) | collective-permute-done | bytes 16416 | tf_op jit(solution)/shard_map/ppermute | solution.py:19
  47.1 0.0 copy-start.3
  47.1 0.0 copy-start.4
  47.1 4.8 %fusion.17 = f32[512,128]{1,0:T(8,128)} fusion(f32[544,128]{1,0:T(8,128)S(1)} %constant_dynamic-update-slice_fusion.2, f32[544,128]{1,0:T(8,128)S(1)} %get-tuple-element.23, f32[512,128]{1,0:T(8,128)} %reduce-scatter.2.cloned.1.call-done, s32[128]{0:T(128)S(1)} %get-tuple-element.10, s32[512]{0:T(512)S(1)} %iota_add_fusion, ...), kind=kLoop, calls=%fused_computation.37 | loop fusion | flops 9109504 | bytes 17308288 | tf_op jit(solution)/shard_map/rsqrt | solution.py:42
  51.9 0.0 all-gather.2.cloned.1.call-update
  52.0 0.0 all-reduce.3.cloned.1.call-start
  52.0 0.0 copy-done.3
  52.0 0.7 fusion.83
  57.8 0.0 copy-done.4
  57.8 0.6 fusion.82
  63.5 5.5 %all-gather.2.cloned.1.call-done = f32[512,512]{1,0:T(8,128)} async-done(((f32[512,128]{1,0:T(8,128)}), f32[512,512]{1,0:T(8,128)}) %all-gather.2.cloned.1.call-update) | async-done | bytes 1048592 | tf_op jit(solution)/shard_map/all_gather | solution.py:56
  68.9 2.3 fusion.1
  71.2 3.1 %dynamic-slice_select_fusion.3 = (bf16[2,2,256,512]{3,2,1,0:T(8,128)(2,1)}, bf16[2,2,256,512]{3,2,1,0:T(8,128)(2,1)}, bf16[2,2,256,512]{3,2,1,0:T(8,128)(2,1)}, bf16[2,2,256,512]{3,2,1,0:T(8,128)(2,1)}) fusion(bf16[2,2,512,512]{3,2,1,0:T(8,128)(2,1)S(1)} %fusion.1, s32[]{:T(128)S(6)} %select_n.304, pred[]{:T(512)S(6)} %eq.12, s32[]{:T(128)S(6)} %select_n.313, ...), kind=kLoop, calls=%fused_computation.32 | loop fusion | flops 2097152 | bytes 8388628 | tf_op jit(solution)/shard_map/jit(_where)/select_n | solution.py:25
  74.4 0.0 all-reduce.3.cloned.1.call-update
  74.4 156.6 %all-reduce.3.cloned.1.call-done = (bf16[2,512,512]{2,1,0:T(8,128)(2,1)}, bf16[2,512,512]{2,1,0:T(8,128)(2,1)}, bf16[2,512,512]{2,1,0:T(8,128)(2,1)}, bf16[2,512,512]{2,1,0:T(8,128)(2,1)}) async-done(((bf16[2,512,512]{2,1,0:T(8,128)(2,1)}, bf16[2,512,512]{2,1,0:T(8,128)(2,1)}, bf16[2,512,512]{2,1,0:T(8,128)(2,1)}, bf16[2,512,512]{2,1,0:T(8,128)(2,1)}), (bf16[2,512,512]{2,1,0:T(8,128)(2,1)}, ...) | async-done | bytes 4194320 | tf_op jit(solution)/shard_map/psum | solution.py:26
  231.0 2.5 fusion.87
  233.5 0.0 copy-start.2
  233.5 0.3 fusion.7
  233.8 0.9 copy-done.2
  234.7 1.3 fusion.86
  236.0 0.0 copy-start.1
  236.0 0.3 fusion.9
  236.3 0.9 copy-done.1
  237.3 1.3 fusion.85
  238.5 0.0 copy-start
  238.6 0.3 fusion.11
  238.8 0.9 copy-done
  239.8 1.3 fusion.84
  241.1 0.3 fusion.13
  241.3 0.5 fusion.4
  241.9 0.5 fusion.2
  242.4 0.6 pad_maximum_fusion
  243.0 2.3 copy.5
  (4 shorter events, 0.0 us)
Async XLA Ops:
  6.5 30.9 %reduce-scatter.2.cloned.1.call-start = ((), (), s32[]{:S(2)}) async-start(), calls=%async_computation.1 | async-start | bytes 1310720 | tf_op jit(solution)/shard_map/reduce_scatter | solution.py:52
  9.7 59.3 %all-gather.2.cloned.1.call-start = ((), (), s32[]{:S(2)}) async-start(), calls=%async_computation.2 | async-start | bytes 1310720 | tf_op jit(solution)/shard_map/all_gather | solution.py:56
  38.1 4.8 %collective-permute-start = (f32[32,128]{1,0:T(8,128)S(1)}, f32[32,128]{1,0:T(8,128)S(1)}, u32[]{:S(2)}, u32[]{:S(2)}) collective-permute-start(f32[32,128]{1,0:T(8,128)S(1)} %get-tuple-element.25), channel_id=1, source_target_pairs={{0,4},{4,8},{8,12},{12,16},{16,20},{20,24},{24,28},{1,5},{5,9},{9,... | collective-permute-start | bytes 49160 | tf_op jit(solution)/shard_map/ppermute | solution.py:16
  41.5 5.6 %collective-permute-start.1 = (f32[32,128]{1,0:T(8,128)S(1)}, f32[32,128]{1,0:T(8,128)S(1)}, u32[]{:S(2)}, u32[]{:S(2)}) collective-permute-start(f32[32,128]{1,0:T(8,128)S(1)} %get-tuple-element.26), channel_id=1, source_target_pairs={{4,0},{8,4},{12,8},{16,12},{20,16},{24,20},{28,24},{5,1},{9,5},{13... | collective-permute-start | bytes 49160 | tf_op jit(solution)/shard_map/ppermute | solution.py:19
  47.1 4.9 %copy-start.3 = (s32[4]{0:T(128)S(1)}, s32[4]{0:T(128)}, u32[]{:S(2)}) copy-start(s32[4]{0:T(128)} %param.7) | copy-start | bytes 52
  47.1 10.7 %copy-start.4 = (s32[4]{0:T(128)S(1)}, s32[4]{0:T(128)}, u32[]{:S(2)}) copy-start(s32[4]{0:T(128)} %param.6) | copy-start | bytes 52
  52.0 179.1 %all-reduce.3.cloned.1.call-start = ((), (), s32[]{:S(2)}) async-start(), calls=%async_computation.3 | async-start | bytes 8388608 | tf_op jit(solution)/shard_map/psum | solution.py:26
  233.5 1.2 copy-start.2
  236.0 1.2 copy-start.1
  238.5 1.2 copy-start
Sparse Core Ops, SparseCore 0:
  9.9 27.4 reduce-scatter.1
  52.1 16.8 all-gather.1
  74.5 156.4 all-reduce.2
where the time goes:
time: 252 us
  waiting for transfers between devices  192 us (76%)
  between operations  23.4 us (9%)
  other arithmetic  16.8 us (7%)
  local copies, waits for them, and re-layouts  8.2 us (3%)
  matrix products  6.34 us (3%)
  starting transfers between devices  4.72 us (2%)
    psum x1, waiting for transfers between devices, from_root(): return lax.psum(block, axis)  157 us
    reduce_scatter x1, waiting for transfers between devices, local(): lax.psum_scatter(local_power, 'band', scatter_dimension=1, tiled=True)  26.9 us
    dot_general x4, matrix products, local(): jnp.einsum('fxw,fyw->fxy', flat, right, preferred_element_type=jnp.float32)  6.34 us
    all_gather x1, waiting for transfers between devices, local(): scale = lax.all_gather(scale_share, 'band', axis=1, tiled=True)  5.46 us
  transfers between devices with their start and end apart: 5, of which 5 were waited for; matrix products, arithmetic and copies ran while one was open for 1% of the time, Pallas kernels for 0%

commit v1 on v0

--- a/solution.py
+++ b/solution.py
@@ -23,7 +23,7 @@
 
 def from_root(block, axis, holder):
     block = jnp.where(lax.axis_index(axis) == holder, block, jnp.zeros_like(block))
-    return lax.psum(block, axis)
+    return jnp.sum(jax.lax.all_gather(block, axis_name=axis), axis=0)
 
 
 def norm_scale(power, widths, first_chan, channels, bins):

time: 252 us -> 600 us (2.38)
  waiting for transfers between devices: 192 us -> 517 us
  other arithmetic: 16.8 us -> 39.7 us
    all_gather x0 -> x4, waiting for transfers between devices: none -> 480 us  [from_root(): return jnp.sum(jax.lax.all_gather(block, axis_name=axis), axis=0)]
    psum x1 -> x0, waiting for transfers between devices: 157 us -> none  [from_root(): return lax.psum(block, axis)]
    reduce_sum x0 -> x4, other arithmetic: none -> 22.8 us  [from_root(): return jnp.sum(jax.lax.all_gather(block, axis_name=axis), axis=0)]
  transfers between devices with their start and end apart: 5 -> 8, of which waited for: 5 -> 8; matrix products, arithmetic and copies ran while one was open for 1% -> 3% of each run, Pallas kernels for 0% -> 0%
where the time goes in v1:
time: 600 us; the launch traced here: 599 us
  waiting for transfers between devices  517 us (86%)
  other arithmetic  39.7 us (7%)
  between operations  23.6 us (4%)
  local copies, waits for them, and re-layouts  7.24 us (1%)
  matrix products  6.34 us (1%)
    all_gather x4, waiting for transfers between devices, from_root(): return jnp.sum(jax.lax.all_gather(block, axis_name=axis), axis=0)  480 us
    reduce_scatter x1, waiting for transfers between devices, local(): lax.psum_scatter(local_power, 'band', scatter_dimension=1, tiled=True)  26.9 us
    reduce_sum x4, other arithmetic, from_root(): return jnp.sum(jax.lax.all_gather(block, axis_name=axis), axis=0)  22.8 us
  transfers between devices with their start and end apart: 8, of which 8 were waited for; matrix products, arithmetic and copies ran while one was open for 3% of the time, Pallas kernels for 0%

profile of v1, /device:TPU:0, one launch (start us, length us, event | category | flops | bytes accessed | tf_op | source)
XLA Modules:
  0.0 599.3 jit_solution(13967705262658236777)
XLA Ops:
  6.5 3.1 fusion
  9.6 0.0 reduce-scatter.2.cloned.1.call-update
  9.7 0.0 all-gather.10.cloned.1.call-start
  9.7 0.8 broadcast_compare_fusion.32
  10.5 26.9 %reduce-scatter.2.cloned.1.call-done = f32[512,128]{1,0:T(8,128)} async-done(((f32[512,512]{1,0:T(8,128)}), f32[512,128]{1,0:T(8,128)}) %reduce-scatter.2.cloned.1.call-update) | async-done | bytes 262160 | tf_op jit(solution)/shard_map/reduce_scatter | solution.py:52
  37.4 0.7 fusion.81
  38.1 3.3 collective-permute-start
  41.5 1.3 collective-permute-start.1
  42.8 0.1 collective-permute-done
  42.9 1.0 constant_dynamic-update-slice_fusion
  43.9 3.2 collective-permute-done.1
  47.1 4.8 fusion.17
  51.9 0.0 all-gather.10.cloned.1.call-update
  52.0 0.0 all-gather.12.cloned.1.call-start
  52.0 0.7 fusion.83
  57.7 0.7 fusion.82
  63.3 5.6 all-gather.10.cloned.1.call-done
  68.9 2.3 fusion.1
  71.2 3.1 dynamic-slice_select_fusion.3
  74.4 0.0 all-gather.12.cloned.1.call-update
  74.4 0.0 all-gather.18.cloned.1.call-start
  74.4 0.5 all-gather.18.cloned.1.call-update
  75.0 0.0 all-gather.16.cloned.1.call-start
  75.0 0.5 all-gather.16.cloned.1.call-update
  75.6 0.2 all-gather.14.cloned.1.call-start
  75.8 0.3 all-gather.14.cloned.1.call-update
  76.1 122.9 %all-gather.12.cloned.1.call-done = bf16[16,2,256,512]{3,2,1,0:T(8,128)(2,1)} async-done(((bf16[2,2,256,512]{3,2,1,0:T(8,128)(2,1)}), bf16[16,2,256,512]{3,2,1,0:T(8,128)(2,1)}) %all-gather.12.cloned.1.call-update) | async-done | bytes 8388624 | tf_op jit(solution)/shard_map/all_gather | solution.py:26
  199.0 4.8 reduce_sum.58
  203.8 119.9 %all-gather.18.cloned.1.call-done = bf16[16,2,256,512]{3,2,1,0:T(8,128)(2,1)} async-done(((bf16[2,2,256,512]{3,2,1,0:T(8,128)(2,1)}), bf16[16,2,256,512]{3,2,1,0:T(8,128)(2,1)}) %all-gather.18.cloned.1.call-update) | async-done | bytes 8388624 | tf_op jit(solution)/shard_map/all_gather | solution.py:26
  323.7 6.0 %reduce_sum.61 = bf16[2,2,256,512]{3,2,1,0:T(8,128)(2,1)} reduce(bf16[8,2,2,256,512]{4,3,2,1,0:T(8,128)(2,1)} %bitcast.46, bf16[]{:T(256)} %constant.96.clone.1), dimensions={0}, to_apply=%region_5.6 | reduce | flops 3670016 | bytes 9437186 | tf_op jit(solution)/shard_map/reduce_sum | solution.py:26
  329.7 118.6 %all-gather.16.cloned.1.call-done = bf16[16,2,256,512]{3,2,1,0:T(8,128)(2,1)} async-done(((bf16[2,2,256,512]{3,2,1,0:T(8,128)(2,1)}), bf16[16,2,256,512]{3,2,1,0:T(8,128)(2,1)}) %all-gather.16.cloned.1.call-update) | async-done | bytes 8388624 | tf_op jit(solution)/shard_map/all_gather | solution.py:26
  448.3 6.0 reduce_sum.60
  454.3 118.7 %all-gather.14.cloned.1.call-done = bf16[16,2,256,512]{3,2,1,0:T(8,128)(2,1)} async-done(((bf16[2,2,256,512]{3,2,1,0:T(8,128)(2,1)}), bf16[16,2,256,512]{3,2,1,0:T(8,128)(2,1)}) %all-gather.14.cloned.1.call-update) | async-done | bytes 8388624 | tf_op jit(solution)/shard_map/all_gather | solution.py:26
  573.0 6.0 %reduce_sum.59 = bf16[2,2,256,512]{3,2,1,0:T(8,128)(2,1)} reduce(bf16[8,2,2,256,512]{4,3,2,1,0:T(8,128)(2,1)} %bitcast.48, bf16[]{:T(256)} %constant.96.clone.1), dimensions={0}, to_apply=%region_3.4 | reduce | flops 3670016 | bytes 9437186 | tf_op jit(solution)/shard_map/reduce_sum | solution.py:26
  579.1 2.5 fusion.85
  581.6 0.3 fusion.11
  581.8 0.9 copy-done.1
  582.8 1.3 fusion.86
  584.1 0.3 fusion.9
  584.4 0.9 copy-done
  585.3 1.3 fusion.87
  586.6 0.3 fusion.7
  586.9 1.3 fusion.84
  588.1 0.3 fusion.13
  588.4 0.5 fusion.4
  589.0 0.6 fusion.2
  589.5 0.6 pad_maximum_fusion
  590.1 2.3 copy.6
  (11 shorter events, 0.0 us)
Async XLA Ops:
  6.5 30.9 %reduce-scatter.2.cloned.1.call-start = ((), (), s32[]{:S(2)}) async-start(), calls=%async_computation.1 | async-start | bytes 1310720 | tf_op jit(solution)/shard_map/reduce_scatter | solution.py:52
  9.7 59.3 %all-gather.10.cloned.1.call-start = ((), (), s32[]{:S(2)}) async-start(), calls=%async_computation.2 | async-start | bytes 1310720 | tf_op jit(solution)/shard_map/all_gather | solution.py:56
  38.1 4.8 collective-permute-start
  41.5 5.6 collective-permute-start.1
  47.1 4.9 copy-start.2
  47.1 10.5 %copy-start.3 = (s32[4]{0:T(128)S(1)}, s32[4]{0:T(128)}, u32[]{:S(2)}) copy-start(s32[4]{0:T(128)} %param.6) | copy-start | bytes 52
  52.0 147.0 %all-gather.12.cloned.1.call-start = ((), (), s32[]{:S(2)}) async-start(), calls=%async_computation.3 | async-start | bytes 9437184 | tf_op jit(solution)/shard_map/all_gather | solution.py:26
  74.4 249.3 %all-gather.18.cloned.1.call-start = ((), (), s32[]{:S(2)}) async-start(), calls=%async_computation.6 | async-start | bytes 9437184 | tf_op jit(solution)/shard_map/all_gather | solution.py:26
  75.0 373.4 %all-gather.16.cloned.1.call-start = ((), (), s32[]{:S(2)}) async-start(), calls=%async_computation.5 | async-start | bytes 9437184 | tf_op jit(solution)/shard_map/all_gather | solution.py:26
  75.6 497.5 %all-gather.14.cloned.1.call-start = ((), (), s32[]{:S(2)}) async-start(), calls=%async_computation.4 | async-start | bytes 9437184 | tf_op jit(solution)/shard_map/all_gather | solution.py:26
  581.6 1.2 copy-start.1
  584.1 1.2 copy-start
Sparse Core Ops, SparseCore 0:
  9.9 27.4 reduce-scatter.1
  52.1 16.8 all-gather.9
  74.5 124.4 all-gather.11
  201.0 122.6 all-gather.17
  325.6 122.6 all-gather.15
  450.3 122.6 all-gather.13
